TPU v7x, 32 devices: a whole 2x2x4 slice. The times are simulated.
32 devices in a mesh: dp: 8 (over y, x, core), head: 4 (over z).
Axes of the slice: x: 2, y: 2, z: 4, core: 2. Of those that a mesh axis runs over, the one named last changes fastest.
Arguments:
- tokens: bfloat16 [2048, 2048], P('dp'), may hold values from -6 to 6
- weights: bfloat16 [4, 768, 2048], P('head', 'dp'), may hold values from -0.13479223 to 0.13479223, as said below
- query_gain: float32 [128], replicated, may hold values from 0.25 to 1.75
- key_gain: float32 [128], replicated, may hold values from 0.25 to 1.75
- first_row: int32 [2048], P('dp'), may hold values from 0 to 2047, as said below
- cotangent: bfloat16 [2048, 2048], P('dp', 'head'), may hold values from -6 to 6
Outputs:
- attended: bfloat16 [2048, 2048], P('dp', 'head')
- token_grad: bfloat16 [2048, 2048], P('dp', 'head')
- weight_grad: float32 [4, 768, 2048], P('head', 'dp')
Inputs may be any that keep to these rules, and one draw needn't show every extreme that they name: first_row[i] is the position of the first row of row i's document: documents are runs of consecutive rows, each at most 512 rows long, one of exactly 512 rows, and the last row begins a document of its own. For every even g, weights[g] and weights[g + 1] are equal in their last 256 rows: each key-value head is held by two head devices.
All inputs are finite; a program needn't handle non-finite values.
Results may differ from a plain program's by a relative error of at most 0.017.
Values may be sent and summed in bfloat16 or wider, within the bound.
No kernel may reach another device: no remote copies, remote signals or barrier semaphores. Data moves between devices by JAX's collectives and lax.ppermute only.
A program may use at most 64 MiB of HBM per device.

v0:
```python
import math
import jax
import jax.numpy as jnp
from jax import lax
from jax.sharding import PartitionSpec as P

HD = 128
QH_DEV = 4
COLS = 768
ROWS = 256
SPAN = 2
EPSILON = 1e-06
THETA = 1000000.0
STRETCH = 0.25


def from_behind(x, axis, by):
    devices = lax.axis_size(axis)
    pairs = [(i, i + by) for i in range(devices) if 0 <= i + by < devices]
    return lax.ppermute(x, axis, pairs)


def partner(x, axis, apart):
    return lax.ppermute(x, axis, [(i, i ^ 1 << apart) for i in range(lax.axis_size(axis))])


def rope_tables(position, head_size):
    middle = head_size // 2
    channel = jnp.arange(middle, dtype=jnp.float32)
    frequency = THETA ** (-2.0 * channel / head_size)
    angles = (position.astype(jnp.float32) * STRETCH)[:, None] * frequency[None, :]
    angles = jnp.concatenate([angles, angles], axis=1)
    return (jnp.cos(angles), jnp.sin(angles))


def normalize_rotate(values, scaling, cosine_table, sine_table):
    factor = lax.rsqrt(jnp.mean(values * values, axis=-1, keepdims=True) + EPSILON)
    normed = values * factor * scaling
    middle = normed.shape[-1] // 2
    turned = jnp.concatenate([-normed[..., middle:], normed[..., :middle]], axis=-1)
    return normed * cosine_table + turned * sine_table


def prepare(projected, query_gain, key_gain, cosine_table, sine_table):
    row_count = projected.shape[0]
    queries = projected[:, : QH_DEV * HD].reshape(row_count, QH_DEV, HD)
    queries = normalize_rotate(
        queries, query_gain, cosine_table[:, None, :], sine_table[:, None, :]
    )
    key_part = normalize_rotate(
        projected[:, QH_DEV * HD : (QH_DEV + 1) * HD], key_gain, cosine_table, sine_table
    )
    value_part = projected[:, (QH_DEV + 1) * HD :]
    return (queries, key_part, value_part)


def attend_window(queries, window, upstream, first_rows, query_place, key_place):
    score_scale = 1.0 / math.sqrt(HD)
    key_window = window[:, :HD]
    value_window = window[:, HD:]
    visible = (key_place[None, :] >= first_rows[:, None]) & (
        key_place[None, :] <= query_place[:, None]
    )
    score = (
        jnp.einsum("rhc,kc->rhk", queries, key_window, preferred_element_type=jnp.float32)
        * score_scale
    )
    weight = jnp.where(visible[:, None, :], jnp.exp(score), 0.0)
    denominator = jnp.sum(weight, axis=-1)
    summed = jnp.einsum(
        "rhk,kc->rhc", weight.astype(jnp.bfloat16), value_window, preferred_element_type=jnp.float32
    )
    attended = (summed / denominator[..., None]).astype(jnp.bfloat16)
    probability = weight / denominator[..., None]
    row_delta = jnp.sum(upstream.astype(jnp.float32) * attended.astype(jnp.float32), axis=-1)
    grad_prob = jnp.einsum(
        "rhc,kc->rhk", upstream, value_window, preferred_element_type=jnp.float32
    )
    grad_score = (probability * (grad_prob - row_delta[..., None]) * score_scale).astype(
        jnp.bfloat16
    )
    grad_query = jnp.einsum(
        "rhk,kc->rhc", grad_score, key_window, preferred_element_type=jnp.float32
    )
    grad_key = jnp.einsum("rhk,rhc->kc", grad_score, queries, preferred_element_type=jnp.float32)
    grad_value = jnp.einsum(
        "rhk,rhc->kc",
        probability.astype(jnp.bfloat16),
        upstream,
        preferred_element_type=jnp.float32,
    )
    return (attended, grad_query, jnp.concatenate([grad_key, grad_value], axis=1))


def body(tokens, weights, query_gain, key_gain, first_row, cotangent):
    block_index = lax.axis_index("dp")
    position = block_index * ROWS + jnp.arange(ROWS, dtype=jnp.int32)
    key_place = (block_index - SPAN) * ROWS + jnp.arange((SPAN + 1) * ROWS, dtype=jnp.int32)
    cosine_table, sine_table = rope_tables(position, HD)
    weight_piece = lax.all_gather(weights, "dp", axis=1, tiled=True)
    projected = jnp.einsum("rd,cd->rc", tokens, weight_piece[0], preferred_element_type=jnp.float32)
    prepared, pullback = jax.vjp(
        lambda values: prepare(values, query_gain, key_gain, cosine_table, sine_table), projected
    )
    queries = prepared[0].astype(jnp.bfloat16)
    key_value = jnp.concatenate([prepared[1], prepared[2]], axis=1).astype(jnp.bfloat16)
    earlier = [from_behind(key_value, "dp", distance) for distance in range(SPAN, 0, -1)]
    window = jnp.concatenate(earlier + [key_value], axis=0)
    upstream = cotangent.reshape(ROWS, QH_DEV, HD)
    attended, grad_query, slot_grads = attend_window(
        queries, window, upstream, first_row, position, key_place
    )
    pair_grad = slot_grads[SPAN * ROWS :]
    for distance in range(1, SPAN + 1):
        slot_index = SPAN - distance
        pair_grad = pair_grad + from_behind(
            slot_grads[slot_index * ROWS : (slot_index + 1) * ROWS].astype(jnp.bfloat16),
            "dp",
            -distance,
        ).astype(jnp.float32)
    grad_projected = pullback((grad_query, pair_grad[:, :HD], pair_grad[:, HD:]))[0].astype(
        jnp.bfloat16
    )
    partial_grad = jnp.dot(grad_projected, weight_piece[0], preferred_element_type=jnp.float32)
    token_grad = lax.psum_scatter(
        partial_grad.astype(jnp.bfloat16), "head", scatter_dimension=1, tiled=True
    )
    shard_rows = COLS // lax.axis_size("dp")
    own_grad = lax.psum_scatter(
        jnp.einsum("rc,rd->cd", grad_projected, tokens, preferred_element_type=jnp.float32),
        "dp",
        scatter_dimension=0,
        tiled=True,
    )
    partner_grad = partner(own_grad.astype(jnp.bfloat16), "head", 0).astype(own_grad.dtype)
    global_rows = block_index * shard_rows + jnp.arange(shard_rows, dtype=jnp.int32)
    shared_rows = global_rows >= QH_DEV * HD
    weight_grad = jnp.where(shared_rows[:, None], own_grad + partner_grad, own_grad)
    return (attended.reshape(ROWS, QH_DEV * HD), token_grad, weight_grad[None])


def solution(mesh):
    in_specs = (P("dp", None), P("head", "dp", None), P(), P(), P("dp"), P("dp", "head"))
    out_specs = (P("dp", "head"), P("dp", "head"), P("head", "dp", None))
    return jax.shard_map(body, mesh=mesh, in_specs=in_specs, out_specs=out_specs, check_vma=False)
```

profile of v0, /device:TPU:0, one launch (start us, length us, event | category | flops | bytes accessed | tf_op | source)
XLA Modules:
  0.0 185.5 jit_solution(12164193166599489742)
XLA Ops:
  8.0 1.8 copy.66
  9.9 1.6 compare_and_fusion
  11.5 33.3 %all-gather.2.cloned.1.call-done = bf16[1,768,2048]{2,1,0:T(8,128)(2,1)} async-done(((bf16[1,96,2048]{2,1,0:T(8,128)(2,1)}), bf16[1,768,2048]{2,1,0:T(8,128)(2,1)}) %all-gather.2.cloned.1.call-update) | async-done | bytes 3145744 | tf_op jit(solution)/shard_map/all_gather | solution.py:100
  44.8 2.9 %fusion.4 = f32[256,768]{1,0:T(8,128)S(1)} fusion(bf16[256,2048]{1,0:T(8,128)(2,1)S(1)} %copy-done, bf16[1,768,2048]{2,1,0:T(8,128)(2,1)} %all-gather.2.cloned.1.call-done), kind=kOutput, calls=%fused_computation.5 | convolution fusion | flops 805306368 | bytes 4980736 | tf_op jit(solution)/shard_map/rd,cd->rc/dot_general | solution.py:101
  48.1 1.3 fusion.39
  50.0 2.8 %collective-permute-start.1 = (bf16[256,256]{1,0:T(8,128)(2,1)}, bf16[256,256]{1,0:T(8,128)(2,1)}, u32[]{:S(2)}, u32[]{:S(2)}) collective-permute-start(bf16[256,256]{1,0:T(8,128)(2,1)} %pad_maximum_fusion.2), channel_id=1, source_target_pairs={{0,4},{4,8},{8,12},{12,16},{16,20},{20,24},{24,28},{1,5},{5,9},{9,... | collective-permute-start | bytes 393224 | tf_op jit(solution)/shard_map/ppermute | solution.py:20
  52.8 3.4 %collective-permute-start = (bf16[256,256]{1,0:T(8,128)(2,1)}, bf16[256,256]{1,0:T(8,128)(2,1)}, u32[]{:S(2)}, u32[]{:S(2)}) collective-permute-start(bf16[256,256]{1,0:T(8,128)(2,1)} %pad_maximum_fusion.2), channel_id=1, source_target_pairs={{0,8},{4,12},{8,16},{12,20},{16,24},{20,28},{1,9},{5,13},{9,17},{1... | collective-permute-start | bytes 393224 | tf_op jit(solution)/shard_map/ppermute | solution.py:20
  57.0 1.0 copy.63
  60.5 1.0 fusion.10
  61.6 1.4 multiply_reduce_fusion.1
  63.0 1.1 fusion.19
  64.1 1.5 fusion.1
  67.8 1.3 collective-permute-start.2
  69.1 1.3 collective-permute-start.3
  71.4 7.2 %collective-permute-done.3 = bf16[256,256]{1,0:T(8,128)(2,1)} collective-permute-done((bf16[256,256]{1,0:T(8,128)(2,1)}, bf16[256,256]{1,0:T(8,128)(2,1)}, u32[]{:S(2)}, u32[]{:S(2)}) %collective-permute-start.3) | collective-permute-done | bytes 131104 | tf_op jit(solution)/shard_map/ppermute | solution.py:20
  78.6 1.1 fusion.35
  81.1 3.7 %fusion.48 = f32[768,2048]{1,0:T(8,128)} fusion(bf16[256,2048]{1,0:T(8,128)(2,1)S(1)} %copy-done, f32[256,512]{1,0:T(8,128)S(1)} %copy.87, f32[256,128]{1,0:T(8,128)S(1)} %add_add_fusion.1, f32[256,128]{1,0:T(8,128)S(1)} %get-tuple-element.23), kind=kOutput, calls=%fused_computation.82 | convolution fusion | flops 805896192 | bytes 8126464 | tf_op jit(solution)/shard_map/rc,rd->cd/dot_general | solution.py:130
  84.9 3.9 %fusion.6 = bf16[256,2048]{1,0:T(8,128)(2,1)} fusion(bf16[1,768,2048]{2,1,0:T(8,128)(2,1)} %all-gather.2.cloned.1.call-done, f32[256,512]{1,0:T(8,128)S(1)} %copy.87, f32[256,128]{1,0:T(8,128)S(1)} %add_add_fusion.1, f32[256,128]{1,0:T(8,128)S(1)} %get-tuple-element.23), kind=kOutput, calls=%fused_computation.8 | convolution fusion | flops 806420480 | bytes 4980736 | tf_op jit(solution)/shard_map/dot_general | solution.py:124
  88.8 59.1 %reduce-scatter.5.cloned.1.call-done = f32[96,2048]{1,0:T(8,128)} async-done(((f32[768,2048]{1,0:T(8,128)}), f32[96,2048]{1,0:T(8,128)}) %reduce-scatter.5.cloned.1.call-update) | async-done | bytes 786448 | tf_op jit(solution)/shard_map/reduce_scatter | solution.py:129
  147.9 1.2 convert_element_type.61
  149.1 1.6 collective-permute-start.4
  151.5 11.0 %collective-permute-done.4 = bf16[96,2048]{1,0:T(8,128)(2,1)S(1)} collective-permute-done((bf16[96,2048]{1,0:T(8,128)(2,1)S(1)}, bf16[96,2048]{1,0:T(8,128)(2,1)S(1)}, u32[]{:S(2)}, u32[]{:S(2)}) %collective-permute-start.4) | collective-permute-done | bytes 393248 | tf_op jit(solution)/shard_map/ppermute | solution.py:24
  162.5 2.2 %fusion.29 = f32[1,96,2048]{2,1,0:T(8,128)} fusion(f32[96,2048]{1,0:T(8,128)} %reduce-scatter.5.cloned.1.call-done, bf16[96,2048]{1,0:T(8,128)(2,1)S(1)} %collective-permute-done.4, pred[96]{0:T(512)(128)(4,1)S(1)} %add_compare_fusion), kind=kLoop, calls=%fused_computation.27 | loop fusion | flops 589824 | bytes 1966176 | tf_op jit(solution)/shard_map/broadcast_in_dim | solution.py:139
  164.7 14.3 %reduce-scatter.3.cloned.1.call-done = bf16[256,512]{1,0:T(8,128)(2,1)} async-done(((bf16[256,2048]{1,0:T(8,128)(2,1)}), bf16[256,512]{1,0:T(8,128)(2,1)}) %reduce-scatter.3.cloned.1.call-update) | async-done | bytes 262160 | tf_op jit(solution)/shard_map/reduce_scatter | solution.py:125
  (61 shorter events, 10.6 us)
Async XLA Ops:
  7.2 37.7 %copy-start = (bf16[256,2048]{1,0:T(8,128)(2,1)S(1)}, bf16[256,2048]{1,0:T(8,128)(2,1)}, u32[]{:S(2)}) copy-start(bf16[256,2048]{1,0:T(8,128)(2,1)} %param.6) | copy-start | bytes 3145732
  7.2 37.6 %all-gather.2.cloned.1.call-start = ((), (), s32[]{:S(2)}) async-start(), calls=%async_computation.2 | async-start | bytes 3538944 | tf_op jit(solution)/shard_map/all_gather | solution.py:100
  7.9 140.0 %reduce-scatter.5.cloned.1.call-start = ((), (), s32[]{:S(2)}) async-start(), calls=%async_computation.4 | async-start | bytes 7077888 | tf_op jit(solution)/shard_map/reduce_scatter | solution.py:129
  9.8 38.1 %copy-start.6 = (f32[128]{0:T(128)S(1)}, f32[128]{0:T(128)}, u32[]{:S(2)}) copy-start(f32[128]{0:T(128)} %param.9) | copy-start | bytes 1540
  47.9 10.4 %copy-start.5 = (f32[128]{0:T(128)S(1)}, f32[128]{0:T(128)}, u32[]{:S(2)}) copy-start(f32[128]{0:T(128)} %param.8) | copy-start | bytes 1540
  50.0 8.5 %collective-permute-start.1 = (bf16[256,256]{1,0:T(8,128)(2,1)}, bf16[256,256]{1,0:T(8,128)(2,1)}, u32[]{:S(2)}, u32[]{:S(2)}) collective-permute-start(bf16[256,256]{1,0:T(8,128)(2,1)} %pad_maximum_fusion.2), channel_id=1, source_target_pairs={{0,4},{4,8},{8,12},{12,16},{16,20},{20,24},{24,28},{1,5},{5,9},{9,... | collective-permute-start | bytes 393224 | tf_op jit(solution)/shard_map/ppermute | solution.py:20
  52.8 6.7 %collective-permute-start = (bf16[256,256]{1,0:T(8,128)(2,1)}, bf16[256,256]{1,0:T(8,128)(2,1)}, u32[]{:S(2)}, u32[]{:S(2)}) collective-permute-start(bf16[256,256]{1,0:T(8,128)(2,1)} %pad_maximum_fusion.2), channel_id=1, source_target_pairs={{0,8},{4,12},{8,16},{12,20},{16,24},{20,28},{1,9},{5,13},{9,17},{1... | collective-permute-start | bytes 393224 | tf_op jit(solution)/shard_map/ppermute | solution.py:20
  58.2 2.3 %copy-start.4 = (pred[256,768]{1,0:T(8,128)(4,1)S(1)}, pred[256,768]{1,0:T(8,128)(4,1)}, u32[]{:S(2)}) copy-start(pred[256,768]{1,0:T(8,128)(4,1)} %compare_and_fusion) | copy-start | bytes 589828
  58.4 3.1 %copy-start.3 = (bf16[256,512]{0,1:T(8,128)(2,1)S(1)}, bf16[256,512]{0,1:T(8,128)(2,1)}, u32[]{:S(2)}) copy-start(bf16[256,512]{0,1:T(8,128)(2,1)} %copy.66) | copy-start | bytes 786436
  64.1 3.0 %copy-start.1 = (f32[768,128]{1,0:T(8,128)}, f32[768,128]{1,0:T(8,128)S(1)}, u32[]{:S(2)}) copy-start(f32[768,128]{1,0:T(8,128)S(1)} %fusion.19) | copy-start | bytes 1179652
  67.8 3.6 %collective-permute-start.2 = (bf16[256,256]{1,0:T(8,128)(2,1)}, bf16[256,256]{1,0:T(8,128)(2,1)}, u32[]{:S(2)}, u32[]{:S(2)}) collective-permute-start(bf16[256,256]{1,0:T(8,128)(2,1)} %get-tuple-element.21), channel_id=1, source_target_pairs={{4,0},{8,4},{12,8},{16,12},{20,16},{24,20},{28,24},{5,1},{9,5},{13... | collective-permute-start | bytes 393224 | tf_op jit(solution)/shard_map/ppermute | solution.py:20
  69.1 9.5 %collective-permute-start.3 = (bf16[256,256]{1,0:T(8,128)(2,1)}, bf16[256,256]{1,0:T(8,128)(2,1)}, u32[]{:S(2)}, u32[]{:S(2)}) collective-permute-start(bf16[256,256]{1,0:T(8,128)(2,1)} %get-tuple-element.22), channel_id=1, source_target_pairs={{8,0},{12,4},{16,8},{20,12},{24,16},{28,20},{9,1},{13,5},{17,9},{2... | collective-permute-start | bytes 393224 | tf_op jit(solution)/shard_map/ppermute | solution.py:20
  84.8 65.8 %copy-start.2 = (bf16[256,4,128]{0,2,1:T(8,128)(2,1)S(1)}, bf16[256,4,128]{0,2,1:T(8,128)(2,1)}, u32[]{:S(2)}) copy-start(bf16[256,4,128]{0,2,1:T(8,128)(2,1)} %get-tuple-element.35) | copy-start | bytes 786436
  84.8 94.1 %reduce-scatter.3.cloned.1.call-start = ((), (), s32[]{:S(2)}) async-start(), calls=%async_computation.3 | async-start | bytes 1310720 | tf_op jit(solution)/shard_map/reduce_scatter | solution.py:125
  149.1 13.5 %collective-permute-start.4 = (bf16[96,2048]{1,0:T(8,128)(2,1)S(1)}, bf16[96,2048]{1,0:T(8,128)(2,1)S(1)}, u32[]{:S(2)}, u32[]{:S(2)}) collective-permute-start(bf16[96,2048]{1,0:T(8,128)(2,1)S(1)} %convert_element_type.61), channel_id=1, source_target_pairs={{0,1},{1,0},{2,3},{3,2},{4,5},{5,4},{6,7},{7,6},{8,9},{9,8},{10,11... | collective-permute-start | bytes 1179656 | tf_op jit(solution)/shard_map/ppermute | solution.py:24
Sparse Core Ops, SparseCore 0:
  9.9 34.8 all-gather.1
  84.9 62.8 reduce-scatter.4
  150.8 28.1 reduce-scatter.2
where the time goes:
time: 186 us
  waiting for transfers between devices  127 us (68%)
  matrix products  16.7 us (9%)
  between operations  14.1 us (8%)
  other arithmetic  11.9 us (6%)
  starting transfers between devices  10.4 us (6%)
  local copies, waits for them, and re-layouts  5.22 us (3%)
    reduce_scatter x1, waiting for transfers between devices, body(): lax.psum_scatter(jnp.einsum('rc,rd->cd', grad_projected, tokens, preferre...  59.1 us
    all_gather x1, waiting for transfers between devices, body(): weight_piece = lax.all_gather(weights, 'dp', axis=1, tiled=True)  33.3 us
    reduce_scatter x1, waiting for transfers between devices, body(): lax.psum_scatter(partial_grad.astype(jnp.bfloat16), 'head', scatter_dimen...  14.3 us
    ppermute x1, waiting for transfers between devices, partner(): lax.ppermute(x, axis, [(i, i ^ 1 << apart) for i in range(lax.axis_size(a...  11 us
    ppermute x4, starting transfers between devices, from_behind(): return lax.ppermute(x, axis, pairs)  8.74 us
    ppermute x4, waiting for transfers between devices, from_behind(): return lax.ppermute(x, axis, pairs)  8.71 us
    dot_general x1, matrix products, body(): jnp.dot(grad_projected, weight_piece[0], preferred_element_type=jnp.float32)  3.86 us
  transfers between devices with their start and end apart: 8, of which 7 were waited for; matrix products, arithmetic and copies ran while one was open for 8% of the time, Pallas kernels for 0%

commit v1 on v0

--- a/solution.py
+++ b/solution.py
@@ -12,6 +12,18 @@
 EPSILON = 1e-06
 THETA = 1000000.0
 STRETCH = 0.25
+
+
+def doubled_up(array, axis, dim):
+    ways, here = (lax.axis_size(axis), lax.axis_index(axis))
+    grown, reach = (array, 1)
+    while reach < ways:
+        theirs = lax.ppermute(grown, axis, [(d, d ^ reach) for d in range(ways)])
+        mine_first = jnp.concatenate([grown, theirs], axis=dim)
+        theirs_first = jnp.concatenate([theirs, grown], axis=dim)
+        grown = jnp.where(here & reach == 0, mine_first, theirs_first)
+        reach = 2 * reach
+    return grown
 
 
 def from_behind(x, axis, by):
@@ -97,7 +109,7 @@
     position = block_index * ROWS + jnp.arange(ROWS, dtype=jnp.int32)
     key_place = (block_index - SPAN) * ROWS + jnp.arange((SPAN + 1) * ROWS, dtype=jnp.int32)
     cosine_table, sine_table = rope_tables(position, HD)
-    weight_piece = lax.all_gather(weights, "dp", axis=1, tiled=True)
+    weight_piece = doubled_up(weights, "dp", 1)
     projected = jnp.einsum("rd,cd->rc", tokens, weight_piece[0], preferred_element_type=jnp.float32)
     prepared, pullback = jax.vjp(
         lambda values: prepare(values, query_gain, key_gain, cosine_table, sine_table), projected

time: 186 us -> 206 us (1.11)
  waiting for transfers between devices: 127 us -> 144 us
  starting transfers between devices: 10.4 us -> 14.7 us
    ppermute x0 -> x3, waiting for transfers between devices: none -> 51.5 us  [doubled_up(): theirs = lax.ppermute(grown, axis, [(d, d ^ reach) for d in range(ways)])]
    all_gather x1 -> x0, waiting for transfers between devices: 33.3 us -> none  [body(): weight_piece = lax.all_gather(weights, 'dp', axis=1, tiled=True)]
    select_n x0 -> x4, other arithmetic: none -> 5.92 us  [doubled_up(): grown = jnp.where(here & reach == 0, mine_first, theirs_first)]
    ppermute x0 -> x3, starting transfers between devices: none -> 5.18 us  [doubled_up(): theirs = lax.ppermute(grown, axis, [(d, d ^ reach) for d in range(ways)])]
  transfers between devices with their start and end apart: 8 -> 10, of which waited for: 7 -> 9; matrix products, arithmetic and copies ran while one was open for 8% -> 6% of each run, Pallas kernels for 0% -> 0%
where the time goes in v1:
time: 206 us
  waiting for transfers between devices  144 us (70%)
  matrix products  16.6 us (8%)
  starting transfers between devices  14.7 us (7%)
  between operations  14.4 us (7%)
  other arithmetic  12.5 us (6%)
  local copies, waits for them, and re-layouts  3.32 us (2%)
    reduce_scatter x1, waiting for transfers between devices, body(): lax.psum_scatter(jnp.einsum('rc,rd->cd', grad_projected, tokens, preferre...  57.9 us
    ppermute x3, waiting for transfers between devices, doubled_up(): theirs = lax.ppermute(grown, axis, [(d, d ^ reach) for d in range(ways)])  51.5 us
    reduce_scatter x1, waiting for transfers between devices, body(): lax.psum_scatter(partial_grad.astype(jnp.bfloat16), 'head', scatter_dimen...  14.3 us
    ppermute x4, waiting for transfers between devices, from_behind(): return lax.ppermute(x, axis, pairs)  10.6 us
    ppermute x1, waiting for transfers between devices, partner(): lax.ppermute(x, axis, [(i, i ^ 1 << apart) for i in range(lax.axis_size(a...  10.1 us
    ppermute x4, starting transfers between devices, from_behind(): return lax.ppermute(x, axis, pairs)  7.88 us
    select_n x4, other arithmetic, doubled_up(): grown = jnp.where(here & reach == 0, mine_first, theirs_first)  5.92 us
    ppermute x3, starting transfers between devices, doubled_up(): theirs = lax.ppermute(grown, axis, [(d, d ^ reach) for d in range(ways)])  5.18 us
  transfers between devices with their start and end apart: 10, of which 9 were waited for; matrix products, arithmetic and copies ran while one was open for 6% of the time, Pallas kernels for 0%

profile of v1, /device:TPU:0, one launch (start us, length us, event | category | flops | bytes accessed | tf_op | source)
XLA Modules:
  0.0 205.9 jit_solution(18116713539613254351)
XLA Ops:
  7.8 1.6 collective-permute-done
  9.3 2.2 %maximum_select_fusion.4 = bf16[1,192,2048]{2,1,0:T(8,128)(2,1)} fusion(bf16[1,96,2048]{2,1,0:T(8,128)(2,1)S(1)} %collective-permute-done, bf16[1,96,2048]{2,1,0:T(8,128)(2,1)} %param.7, pred[]{:T(512)S(6)} %eq.11), kind=kLoop, calls=%fused_computation.29 | loop fusion | flops 3538944 | bytes 1572865 | tf_op jit(solution)/shard_map/jit(_where)/select_n | solution.py:24
  11.6 2.8 %collective-permute-start.1 = (bf16[1,192,2048]{2,1,0:T(8,128)(2,1)}, bf16[1,192,2048]{2,1,0:T(8,128)(2,1)S(1)}, u32[]{:S(2)}, u32[]{:S(2)}) collective-permute-start(bf16[1,192,2048]{2,1,0:T(8,128)(2,1)} %maximum_select_fusion.4), channel_id=1, source_target_pairs={{0,8},{4,12},{8,0},{12,4},{16,24},{20,28},{24,16},{28,20},{1,9},{5... | collective-permute-start | bytes 2359304 | tf_op jit(solution)/shard_map/ppermute | solution.py:21
  14.4 1.4 maximum_select_fusion.3
  15.8 16.7 %collective-permute-done.1 = bf16[1,192,2048]{2,1,0:T(8,128)(2,1)S(1)} collective-permute-done((bf16[1,192,2048]{2,1,0:T(8,128)(2,1)}, bf16[1,192,2048]{2,1,0:T(8,128)(2,1)S(1)}, u32[]{:S(2)}, u32[]{:S(2)}) %collective-permute-start.1) | collective-permute-done | bytes 786464 | tf_op jit(solution)/shard_map/ppermute | solution.py:21
  32.5 1.7 maximum_select_fusion.2
  34.2 1.8 collective-permute-start.2
  37.1 33.3 %collective-permute-done.2 = bf16[1,384,2048]{2,1,0:T(8,128)(2,1)} collective-permute-done((bf16[1,384,2048]{2,1,0:T(8,128)(2,1)}, bf16[1,384,2048]{2,1,0:T(8,128)(2,1)}, u32[]{:S(2)}, u32[]{:S(2)}) %collective-permute-start.2) | collective-permute-done | bytes 1572896 | tf_op jit(solution)/shard_map/ppermute | solution.py:21
  70.4 2.9 %convolution_bitcast_fusion = f32[256,768]{0,1:T(8,128)S(1)} fusion(bf16[256,2048]{1,0:T(8,128)(2,1)S(1)} %copy-done, bf16[384,2048]{1,0:T(8,128)(2,1)} %bitcast.4, bf16[384,2048]{1,0:T(8,128)(2,1)S(1)} %maximum_select_fusion.1, pred[]{:T(512)S(6)} %eq.9), kind=kOutput, calls=%fused_computation.17 | convolution fusion | flops 819462144 | bytes 4980737 | tf_op jit(solution)/shard_map/rd,cd->rc/dot_general | solution.py:113
  74.1 1.3 collective-permute-start.4
  75.4 4.0 %collective-permute-start.3 = (bf16[256,256]{0,1:T(8,128)(2,1)S(1)}, bf16[256,256]{0,1:T(8,128)(2,1)S(1)}, u32[]{:S(2)}, u32[]{:S(2)}) collective-permute-start(bf16[256,256]{0,1:T(8,128)(2,1)S(1)} %pad_maximum_fusion.2), channel_id=1, source_target_pairs={{0,8},{4,12},{8,16},{12,20},{16,24},{20,28},{1,9},{5,13},{9,17},{1... | collective-permute-start | bytes 393224 | tf_op jit(solution)/shard_map/ppermute | solution.py:32
  79.8 2.9 %collective-permute-done.3 = bf16[256,256]{0,1:T(8,128)(2,1)S(1)} collective-permute-done((bf16[256,256]{0,1:T(8,128)(2,1)S(1)}, bf16[256,256]{0,1:T(8,128)(2,1)S(1)}, u32[]{:S(2)}, u32[]{:S(2)}) %collective-permute-start.3) | collective-permute-done | bytes 131104 | tf_op jit(solution)/shard_map/ppermute | solution.py:32
  83.7 1.5 multiply_reduce_fusion.1
  86.3 1.4 fusion.1
  92.5 7.0 %collective-permute-done.6 = bf16[256,256]{0,1:T(8,128)(2,1)S(1)} collective-permute-done((bf16[256,256]{0,1:T(8,128)(2,1)S(1)}, bf16[256,256]{0,1:T(8,128)(2,1)S(1)}, u32[]{:S(2)}, u32[]{:S(2)}) %collective-permute-start.6) | collective-permute-done | bytes 131104 | tf_op jit(solution)/shard_map/ppermute | solution.py:32
  101.0 3.6 %fusion.43 = f32[768,2048]{1,0:T(8,128)} fusion(bf16[256,2048]{1,0:T(8,128)(2,1)S(1)} %copy-done, f32[256,512]{0,1:T(8,128)S(1)} %bitcast.56, f32[256,128]{0,1:T(8,128)S(1)} %add_add_fusion.1, f32[256,128]{0,1:T(8,128)S(1)} %get-tuple-element.12), kind=kOutput, calls=%fused_computation.86 | convolution fusion | flops 805896192 | bytes 8126464 | tf_op jit(solution)/shard_map/rc,rd->cd/dot_general | solution.py:142
  104.7 1.3 copy-done.2
  106.0 4.0 %convolution_convert_fusion = bf16[256,2048]{1,0:T(8,128)(2,1)} fusion(bf16[384,2048]{1,0:T(8,128)(2,1)} %bitcast.4, bf16[384,2048]{1,0:T(8,128)(2,1)S(1)} %copy-done.2, pred[]{:T(512)S(6)} %eq.9, f32[256,512]{0,1:T(8,128)S(1)} %bitcast.57, f32[256,128]{0,1:T(8,128)S(1)} %add_add_fusion.1, f32[256,128]{0,1:T(8,128)S(1)} %get-tuple-element.12), kind=kOutput, calls=%fused_computation.5 | convolution fusion | flops 820576256 | bytes 4980737 | tf_op jit(solution)/shard_map/dot_general | solution.py:136
  110.1 57.9 %reduce-scatter.5.cloned.1.call-done = f32[96,2048]{1,0:T(8,128)} async-done(((f32[768,2048]{1,0:T(8,128)}), f32[96,2048]{1,0:T(8,128)}) %reduce-scatter.5.cloned.1.call-update) | async-done | bytes 786448 | tf_op jit(solution)/shard_map/reduce_scatter | solution.py:141
  169.2 1.6 collective-permute-start.7
  170.8 1.8 copy.15
  172.6 10.1 %collective-permute-done.7 = bf16[96,2048]{1,0:T(8,128)(2,1)S(1)} collective-permute-done((bf16[96,2048]{1,0:T(8,128)(2,1)S(1)}, bf16[96,2048]{1,0:T(8,128)(2,1)S(1)}, u32[]{:S(2)}, u32[]{:S(2)}) %collective-permute-start.7) | collective-permute-done | bytes 393248 | tf_op jit(solution)/shard_map/ppermute | solution.py:36
  182.7 2.2 %fusion.22 = f32[1,96,2048]{2,1,0:T(8,128)} fusion(f32[96,2048]{1,0:T(8,128)} %reduce-scatter.5.cloned.1.call-done, bf16[96,2048]{1,0:T(8,128)(2,1)S(1)} %collective-permute-done.7, pred[96]{0:T(512)(128)(4,1)S(1)} %add_compare_fusion), kind=kLoop, calls=%fused_computation.27 | loop fusion | flops 589824 | bytes 1966176 | tf_op jit(solution)/shard_map/broadcast_in_dim | solution.py:151
  184.8 14.3 %reduce-scatter.3.cloned.1.call-done = bf16[256,512]{1,0:T(8,128)(2,1)} async-done(((bf16[256,2048]{1,0:T(8,128)(2,1)}), bf16[256,512]{1,0:T(8,128)(2,1)}) %reduce-scatter.3.cloned.1.call-update) | async-done | bytes 262160 | tf_op jit(solution)/shard_map/reduce_scatter | solution.py:137
  (61 shorter events, 12.3 us)
Async XLA Ops:
  7.2 63.2 %copy-start = (bf16[256,2048]{1,0:T(8,128)(2,1)S(1)}, bf16[256,2048]{1,0:T(8,128)(2,1)}, u32[]{:S(2)}) copy-start(bf16[256,2048]{1,0:T(8,128)(2,1)} %param.6) | copy-start | bytes 3145732
  7.2 160.8 %reduce-scatter.5.cloned.1.call-start = ((), (), s32[]{:S(2)}) async-start(), calls=%async_computation.3 | async-start | bytes 7077888 | tf_op jit(solution)/shard_map/reduce_scatter | solution.py:141
  7.2 2.1 %collective-permute-start = (bf16[1,96,2048]{2,1,0:T(8,128)(2,1)}, bf16[1,96,2048]{2,1,0:T(8,128)(2,1)S(1)}, u32[]{:S(2)}, u32[]{:S(2)}) collective-permute-start(bf16[1,96,2048]{2,1,0:T(8,128)(2,1)} %param.7), channel_id=1, source_target_pairs={{0,4},{4,0},{8,12},{12,8},{16,20},{20,16},{24,28},{28,24},{1,5},{5... | collective-permute-start | bytes 1179656 | tf_op jit(solution)/shard_map/ppermute | solution.py:21
  7.8 28.2 %copy-start.3 = (bf16[256,512]{1,0:T(8,128)(2,1)S(1)}, bf16[256,512]{1,0:T(8,128)(2,1)}, u32[]{:S(2)}) copy-start(bf16[256,512]{1,0:T(8,128)(2,1)} %param.11) | copy-start | bytes 786436
  7.8 28.5 %copy-start.6 = (s32[256]{0:T(256)S(1)}, s32[256]{0:T(256)}, u32[]{:S(2)}) copy-start(s32[256]{0:T(256)} %param.10) | copy-start | bytes 3076
  11.6 20.9 %collective-permute-start.1 = (bf16[1,192,2048]{2,1,0:T(8,128)(2,1)}, bf16[1,192,2048]{2,1,0:T(8,128)(2,1)S(1)}, u32[]{:S(2)}, u32[]{:S(2)}) collective-permute-start(bf16[1,192,2048]{2,1,0:T(8,128)(2,1)} %maximum_select_fusion.4), channel_id=1, source_target_pairs={{0,8},{4,12},{8,0},{12,4},{16,24},{20,28},{24,16},{28,20},{1,9},{5... | collective-permute-start | bytes 2359304 | tf_op jit(solution)/shard_map/ppermute | solution.py:21
  34.2 36.2 %collective-permute-start.2 = (bf16[1,384,2048]{2,1,0:T(8,128)(2,1)}, bf16[1,384,2048]{2,1,0:T(8,128)(2,1)}, u32[]{:S(2)}, u32[]{:S(2)}) collective-permute-start(bf16[1,384,2048]{2,1,0:T(8,128)(2,1)} %maximum_select_fusion.2), channel_id=1, source_target_pairs={{0,16},{4,20},{8,24},{12,28},{16,0},{20,4},{24,8},{28,12},{1,17},{... | collective-permute-start | bytes 4718600 | tf_op jit(solution)/shard_map/ppermute | solution.py:21
  37.1 36.2 %copy-start.1 = (bf16[384,2048]{1,0:T(8,128)(2,1)}, bf16[384,2048]{1,0:T(8,128)(2,1)S(1)}, u32[]{:S(2)}) copy-start(bf16[384,2048]{1,0:T(8,128)(2,1)S(1)} %maximum_select_fusion.1) | copy-start | bytes 4718596
  70.4 3.1 %copy-start.5 = (f32[128]{0:T(128)S(1)}, f32[128]{0:T(128)}, u32[]{:S(2)}) copy-start(f32[128]{0:T(128)} %param.9) | copy-start | bytes 1540
  70.4 9.0 %copy-start.4 = (f32[128]{0:T(128)S(1)}, f32[128]{0:T(128)}, u32[]{:S(2)}) copy-start(f32[128]{0:T(128)} %param.8) | copy-start | bytes 1540
  74.1 5.7 %collective-permute-start.4 = (bf16[256,256]{0,1:T(8,128)(2,1)S(1)}, bf16[256,256]{0,1:T(8,128)(2,1)S(1)}, u32[]{:S(2)}, u32[]{:S(2)}) collective-permute-start(bf16[256,256]{0,1:T(8,128)(2,1)S(1)} %pad_maximum_fusion.2), channel_id=1, source_target_pairs={{0,4},{4,8},{8,12},{12,16},{16,20},{20,24},{24,28},{1,5},{5,9},{9,... | collective-permute-start | bytes 393224 | tf_op jit(solution)/shard_map/ppermute | solution.py:32
  75.4 7.2 %collective-permute-start.3 = (bf16[256,256]{0,1:T(8,128)(2,1)S(1)}, bf16[256,256]{0,1:T(8,128)(2,1)S(1)}, u32[]{:S(2)}, u32[]{:S(2)}) collective-permute-start(bf16[256,256]{0,1:T(8,128)(2,1)S(1)} %pad_maximum_fusion.2), channel_id=1, source_target_pairs={{0,8},{4,12},{8,16},{12,20},{16,24},{20,28},{1,9},{5,13},{9,17},{1... | collective-permute-start | bytes 393224 | tf_op jit(solution)/shard_map/ppermute | solution.py:32
  89.0 3.5 %collective-permute-start.5 = (bf16[256,256]{0,1:T(8,128)(2,1)S(1)}, bf16[256,256]{0,1:T(8,128)(2,1)S(1)}, u32[]{:S(2)}, u32[]{:S(2)}) collective-permute-start(bf16[256,256]{0,1:T(8,128)(2,1)S(1)} %get-tuple-element.10), channel_id=1, source_target_pairs={{4,0},{8,4},{12,8},{16,12},{20,16},{24,20},{28,24},{5,1},{9,5},{13... | collective-permute-start | bytes 393224 | tf_op jit(solution)/shard_map/ppermute | solution.py:32
  90.3 9.2 %collective-permute-start.6 = (bf16[256,256]{0,1:T(8,128)(2,1)S(1)}, bf16[256,256]{0,1:T(8,128)(2,1)S(1)}, u32[]{:S(2)}, u32[]{:S(2)}) collective-permute-start(bf16[256,256]{0,1:T(8,128)(2,1)S(1)} %get-tuple-element.11), channel_id=1, source_target_pairs={{8,0},{12,4},{16,8},{20,12},{24,16},{28,20},{9,1},{13,5},{17,9},{2... | collective-permute-start | bytes 393224 | tf_op jit(solution)/shard_map/ppermute | solution.py:32
  104.6 1.4 copy-start.2
  104.6 94.5 %reduce-scatter.3.cloned.1.call-start = ((), (), s32[]{:S(2)}) async-start(), calls=%async_computation.2 | async-start | bytes 1310720 | tf_op jit(solution)/shard_map/reduce_scatter | solution.py:137
  169.2 13.5 %collective-permute-start.7 = (bf16[96,2048]{1,0:T(8,128)(2,1)S(1)}, bf16[96,2048]{1,0:T(8,128)(2,1)S(1)}, u32[]{:S(2)}, u32[]{:S(2)}) collective-permute-start(bf16[96,2048]{1,0:T(8,128)(2,1)S(1)} %convert_element_type.61), channel_id=1, source_target_pairs={{0,1},{1,0},{2,3},{3,2},{4,5},{5,4},{6,7},{7,6},{8,9},{9,8},{10,11... | collective-permute-start | bytes 1179656 | tf_op jit(solution)/shard_map/ppermute | solution.py:36
Sparse Core Ops, SparseCore 0:
  104.8 63.2 reduce-scatter.4
  170.9 28.1 reduce-scatter.2
